TPU v7x, 32 devices: a whole 2x2x4 slice. The times are simulated.
32 devices in a mesh: dp: 8 (over z, y), group: 4 (over x, core).
Axes of the slice: x: 2, y: 2, z: 4, core: 2. Of those that a mesh axis runs over, the one named last changes fastest.
Arguments:
- query_feats: bfloat16 [4096, 4096], P(('dp', 'group')), may hold values from -45 to 45
- passage_feats: bfloat16 [4096, 4096], P(('dp', 'group')), may hold values from -45 to 45
- head: bfloat16 [4096, 1024], replicated, may hold values from -0.09375 to 0.09375
- neg_ids: int32 [4096, 7], P(('dp', 'group')), may hold values from 0 to 4095, as said below
Outputs:
- head_grad: float32 [4096, 1024], P(('dp', 'group'))
- query_loss: float32 [4096], P(('dp', 'group'))
Inputs may be any that keep to these rules, and one draw needn't show every extreme that they name: `neg_ids`: the 7 ids of a query name rows on 7 different devices, each with the query's group index and another dp index. Of the ids of one device's rows, at most 128 name rows of any one other device, and for every device some other device is named exactly 128 times.
All inputs are finite; a program needn't handle non-finite values.
Results may differ from a plain program's by a relative error of at most 0.0045.
The roundings to bfloat16 on the way count: a program that leaves them out, or rounds other values in their place, can miss the bound.
Values may be sent and summed in bfloat16 or wider, within the bound.
A program may use at most 128 MiB of HBM per device.

v0:
```python
import functools
import math

import jax
import jax.numpy as jnp
from jax import lax
from jax.experimental import pallas as pl
from jax.experimental.pallas import tpu as pltpu
from jax.sharding import PartitionSpec as P

scaling_divisor = 0.05
levels = 15.0
epsilon = 1e-06
MESH = pl.DeviceIdType.MESH
VMEM = pl.BlockSpec(memory_space=pltpu.VMEM)


def quantize(projected, low, stride, inv_stride):
    level = (projected.astype(jnp.float32) - low) * inv_stride
    turn = level - jnp.floor(level + 0.5)
    quarter = 0.25 - jnp.abs(jnp.abs(turn) - 0.25)
    angle = jnp.where(turn < 0, -quarter, quarter) * (2.0 * math.pi)
    square = angle * angle
    series = -1.0 / math.factorial(11)
    for order in (9, 7, 5, 3, 1):
        series = (-1.0) ** (order // 2) / math.factorial(order) + square * series
    return low + stride * (level - angle * series * (1.0 / (2.0 * math.pi)))


def norm_back(cotangent, quantized, inverse):
    inner_prod = jnp.sum(quantized * cotangent, axis=-1, keepdims=True)
    return (inverse * cotangent - quantized * (inverse**3 * inner_prod)).astype(jnp.bfloat16)


def dot_nn(a, b):
    return jnp.dot(a, b, preferred_element_type=jnp.float32)


def dot_nt(a, b):
    return lax.dot_general(a, b, (((1,), (1,)), ((), ())), preferred_element_type=jnp.float32)


def dot_tn(a, b):
    return lax.dot_general(a, b, (((0,), (0,)), ((), ())), preferred_element_type=jnp.float32)


def remote(src, dst, send, recv, device):
    return pltpu.make_async_remote_copy(
        src_ref=src,
        dst_ref=dst,
        send_sem=send,
        recv_sem=recv,
        device_id=device,
        device_id_type=MESH,
    )


def step_kernel(
    n_dp, n_group, inner, chunks,
    proj_query, proj_pass, stats, query_feats, pass_feats, named, out, loss,
    stats_group, stats_dp, stats_mid,
    emb_query, emb_pass, quant_query, quant_pass, inv_query, inv_pass,
    batch_query, batch_pass, dp_query, dp_pass, hard_exp,
    batch_out, batch_in, hard_out, hard_in,
    feats, turned, dy, gathered, total, pair_out, pair_in, line_out, line_in, kept,
    s_stat_g, r_stat_g, s_stat_d, r_stat_d, s_feat, r_feat,
    s_line, s_pair, r_dp, s_batch, r_batch, s_bw, r_bw, s_hw, r_hw,
    s_dy, r_dy, s_p, r_p, s_l, r_l, *staged
):
    me_d, me_g = lax.axis_index("dp"), lax.axis_index("group")
    line = n_dp // inner
    z, y = me_d // inner, lax.rem(me_d, inner)
    rows, emb = proj_query.shape
    wide = emb // chunks
    block = out.shape[0]
    columns = lambda c: pl.ds(c * wide, wide)
    group_at = lambda k: lax.rem(me_g + k, n_group)
    group_from = lambda k: lax.rem(me_g + n_group - k, n_group)
    dp_at = lambda k: lax.rem(me_d + k, n_dp)
    dp_from = lambda k: lax.rem(me_d + n_dp - k, n_dp)

    cut_feats = (staged[0].at[0], staged[0].at[1]) if staged else (query_feats, pass_feats)

    def feat_copy(i, k):
        src = cut_feats[i]
        return remote(
            src.at[group_at(k)], feats.at[i, k], s_feat.at[i, k], r_feat.at[i, k], (me_d, group_at(k))
        )

    def largest(src, landing, send, recv, count, target):
        copies = []
        for k in range(1, count):
            copies.append(remote(src, landing.at[k], send.at[k], recv.at[k], target(k)))
            copies[-1].start()
        value = src[...]
        for k in range(1, count):
            copies[k - 1].wait()
            value = jnp.maximum(value, landing[k])
        return value

    if staged:
        for i, whole in enumerate((query_feats, pass_feats)):
            for d in range(n_dp):
                for g in range(n_group):
                    staged[0][i, g, :, d * block : (d + 1) * block] = whole[
                        :, (d * n_group + g) * block : (d * n_group + g + 1) * block
                    ]

    stats_mid[...] = largest(
        stats, stats_group, s_stat_g, r_stat_g, n_group, lambda k: (me_d, group_at(k))
    )
    for i in range(2):
        for k in range(1, n_group):
            feat_copy(i, k).start()
    bounds = largest(stats_mid, stats_dp, s_stat_d, r_stat_d, n_dp, lambda k: (dp_at(k), me_g))
    high, low = bounds[0:1], -bounds[1:2]
    stride = (high - low) / levels
    inv_stride = 1.0 / stride

    items = ((emb_pass, batch_pass, dp_pass), (emb_query, batch_query, dp_query))

    def slot_copy(i, source, src, send, target):
        return remote(src, items[i][2].at[source], send, r_dp.at[i, source], (target, me_g))

    def forwards(i, at, src, rightward, leftward):
        source = at * inner + y
        copies = []
        if rightward:
            copies.append((z < line - 1, slot_copy(i, source, src, s_line.at[i, 0, at], dp_at(inner))))
        if leftward:
            copies.append((z > 0, slot_copy(i, source, src, s_line.at[i, 1, at], dp_from(inner))))
        for k in range(1, inner):
            target = z * inner + lax.rem(y + k, inner)
            copies.append((None, slot_copy(i, source, src, s_pair.at[i, k, at], target)))
        return copies

    def each(copies, act):
        for condition, copy in copies:
            if condition is None:
                act(copy)
            else:
                pl.when(condition)(functools.partial(act, copy))

    def start(copy):
        copy.start()

    def wait_send(copy):
        copy.wait_send()

    def batch_copy(i, k):
        return remote(
            items[i][0], items[i][1].at[k], s_batch.at[i, k], r_batch.at[i, k], (me_d, group_at(k))
        )

    def start_own(i):
        each(forwards(i, z, items[i][0], True, True), start)
        for k in range(1, n_group):
            batch_copy(i, k).start()

    def relay(i, s):
        for at, inside, onward in ((z - s, z >= s, True), (z + s, z + s < line, False)):

            @pl.when(inside)
            def _(at=at, onward=onward):
                source = at * inner + y
                arrived = items[i][2].at[source]
                slot_copy(i, source, arrived, s_line.at[i, 0, at], me_d).wait_recv()
                each(forwards(i, at, arrived, onward, not onward), start)

    def wait_pairs(i):
        for k in range(1, inner):
            for at in range(line):
                source = at * inner + lax.rem(y + k, inner)
                arrived = items[i][2].at[source]
                slot_copy(i, source, arrived, s_pair.at[i, k, at], me_d).wait_recv()

    def wait_all_sent(i):
        each(forwards(i, z, items[i][0], True, True), wait_send)
        for s in range(1, line):
            for at, inside, onward in ((z - s, z >= s, True), (z + s, z + s < line, False)):

                @pl.when(inside)
                def _(at=at, onward=onward):
                    arrived = items[i][2].at[at * inner + y]
                    each(forwards(i, at, arrived, onward, not onward), wait_send)

    def embed(projected, quant, inverse, emb_ref):
        value = quantize(projected[...], low, stride, inv_stride)
        inv = lax.rsqrt(jnp.sum(value * value, axis=-1, keepdims=True) + epsilon)
        quant[...] = value
        inverse[...] = inv
        emb_ref[...] = (value * inv).astype(jnp.bfloat16)

    embed(proj_pass, quant_pass, inv_pass, emb_pass)
    start_own(0)
    embed(proj_query, quant_query, inv_query, emb_query)
    for s in range(1, line):
        relay(0, s)
    start_own(1)

    for i in range(2):
        for k in range(1, n_group):
            feat_copy(i, k).wait()
        lanes = pl.ds(i * rows, rows)
        turned[0, :, lanes] = cut_feats[i][me_g].T
        for k in range(1, n_group):
            turned[k, :, lanes] = feats[i, k].T

    for k in range(1, n_group):
        batch_copy(0, k).wait()
    wait_pairs(0)
    if line > 1:
        relay(1, 1)

    def over_dp(step, value):
        if n_dp > 16:
            return lax.fori_loop(1, n_dp, step, value)
        for k in range(1, n_dp):
            value = step(k, value)
        return value

    query = emb_query[...]
    eye = (
        lax.broadcasted_iota(jnp.int32, (rows, rows), 0)
        == lax.broadcasted_iota(jnp.int32, (rows, rows), 1)
    ).astype(jnp.float32)
    place = lax.broadcasted_iota(jnp.int32, (rows, rows), 1)
    batch_block = lambda k: emb_pass[...] if k == 0 else batch_pass[k]
    scores = [dot_nt(query, batch_block(k)) / scaling_divisor for k in range(n_group)]
    positive = jnp.sum(scores[0] * eye, axis=1, keepdims=True)
    exp_batch = [jnp.exp(score) for score in scores]
    batch_total = sum(jnp.sum(value, axis=1, keepdims=True) for value in exp_batch)
    exp_pos = jnp.exp(positive)

    def hard_step(k, hard_sum):
        source = dp_at(k)
        score = dot_nt(query, dp_pass[source]) / scaling_divisor
        here = named[:, 0:1] == place + source * rows
        for n in range(1, named.shape[1]):
            here = here | (named[:, n : n + 1] == place + source * rows)
        value = jnp.where(here, jnp.exp(score), 0.0)
        hard_exp[k] = value
        return hard_sum + value

    hard_sum = over_dp(hard_step, jnp.zeros((rows, rows), jnp.float32))
    hard_total = exp_pos + jnp.sum(hard_sum, axis=1, keepdims=True)
    column = jnp.log(batch_total) - positive + jnp.log(hard_total) - positive
    loss[...] = jnp.sum(column * eye, axis=0, keepdims=True)

    def weight_copy(k):
        return remote(
            batch_out.at[k], batch_in.at[k], s_bw.at[k], r_bw.at[k], (me_d, group_from(k))
        )

    def hard_copy(k):
        return remote(hard_out.at[k], hard_in.at[k], s_hw.at[k], r_hw.at[k], (dp_at(k), me_g))

    for k in range(n_group):
        weight = exp_batch[k] / batch_total
        if k == 0:
            weight = weight - eye * (2.0 - exp_pos / hard_total)
        batch_out[k] = weight.astype(jnp.bfloat16)
        if k:
            weight_copy(k).start()

    def hard_send(k, nothing):
        hard_out[k] = (hard_exp[k] / hard_total).astype(jnp.bfloat16)
        hard_copy(k).start()
        return nothing

    over_dp(hard_send, 0)
    if line > 2:
        relay(1, 2)

    grad = dot_nn(batch_out[0], emb_pass[...])
    for k in range(1, n_group):
        grad += dot_nn(batch_out[k], batch_pass[k])
    grad = over_dp(lambda k, value: value + dot_nn(hard_out[k], dp_pass[dp_at(k)]), grad)
    dy[0] = norm_back(grad / scaling_divisor, quant_query[...], inv_query[...])

    def dy_copy(i, c, k):
        return remote(
            dy.at[i, :, columns(c)], gathered.at[k, pl.ds(i * rows, rows), columns(c)],
            s_dy.at[i, c, k], r_dy.at[i, c, k], (me_d, group_at(k)),
        )

    for c in range(chunks):
        for k in range(1, n_group):
            dy_copy(0, c, k).start()
    for s in range(3, line):
        relay(1, s)

    for k in range(1, n_group):
        batch_copy(1, k).wait()
        weight_copy(k).wait()
    grad = dot_tn(batch_out[0], emb_query[...])
    for k in range(1, n_group):
        grad += dot_tn(batch_in[k], batch_query[n_group - k])
    grad = grad / scaling_divisor
    wait_pairs(1)

    def hard_back(k, value):
        hard_copy(k).wait()
        weight = hard_in[k]
        one = jnp.sum(weight.astype(jnp.float32), axis=1, keepdims=True)
        hard = (one * dp_query[dp_from(k)].astype(jnp.float32) * (1.0 / scaling_divisor)).astype(
            jnp.bfloat16
        )
        chosen = jnp.where(weight.astype(jnp.float32) != 0, 1.0, 0.0).astype(jnp.bfloat16)
        return value + dot_tn(chosen, hard)

    dy[1] = norm_back(over_dp(hard_back, grad), quant_pass[...], inv_pass[...])
    for c in range(chunks):
        for k in range(1, n_group):
            dy_copy(1, c, k).start()

    def pair_copy(c, k):
        target = z * inner + lax.rem(y + k, inner)
        return remote(
            pair_out.at[c, k - 1], pair_in.at[c, k - 1], s_p.at[c, k], r_p.at[c, k], (target, me_g)
        )

    def line_copy(c, j):
        target = lax.rem(z + j, line) * inner + y
        return remote(
            line_out.at[c, j], line_in.at[c, j], s_l.at[c, j], r_l.at[c, j], (target, me_g)
        )

    def first(c):
        part = dot_nn(turned[0, :, 0:rows], dy[0, :, columns(c)])
        part += dot_nn(turned[0, :, rows:], dy[1, :, columns(c)])
        for k in range(1, n_group):
            dy_copy(0, c, k).wait()
            dy_copy(1, c, k).wait()
            part += dot_nn(turned[k], gathered[k, :, columns(c)])
        total[c] = part.reshape(n_dp, block, wide)
        for k in range(1, inner):
            for at in range(line):
                pair_out[c, k - 1, at] = total[c, at * inner + lax.rem(y + k, inner)].astype(
                    jnp.bfloat16
                )
            pair_copy(c, k).start()

    def second(c):
        for k in range(1, inner):
            pair_copy(c, k).wait()

        def summed(at):
            value = total[c, at * inner + y]
            for k in range(1, inner):
                value += pair_in[c, k - 1, at].astype(jnp.float32)
            return value

        for j in range(1, line):
            line_out[c, j] = summed(lax.rem(z + j, line)).astype(jnp.bfloat16)
            line_copy(c, j).start()
        kept[c] = summed(z)

    def third(c):
        value = kept[c]
        for j in range(1, line):
            line_copy(c, j).wait()
            value += line_in[c, j].astype(jnp.float32)
        out[:, columns(c)] = value

    for c in range(chunks):
        first(c)
        if c:
            second(c - 1)
    second(chunks - 1)
    for i in range(2):
        wait_all_sent(i)
    for c in range(chunks):
        third(c)


def whole_step(proj_query, proj_pass, stats, query_feats, pass_feats, named, n_dp, n_group, block):
    inner = 2 if n_dp % 2 == 0 else 1
    line = n_dp // inner
    rows, emb = proj_query.shape
    depth = n_dp * block
    inside = query_feats.ndim == 2
    chunks = max(1, emb // 256)
    wide = emb // chunks
    bf16 = lambda *shape: pltpu.VMEM(shape, jnp.bfloat16)
    f32 = lambda *shape: pltpu.VMEM(shape, jnp.float32)
    sems = lambda *shape: [pltpu.SemaphoreType.DMA(shape)]
    pairs = lambda *shape: sems(*shape) * 2
    return pl.pallas_call(
        functools.partial(step_kernel, n_dp, n_group, inner, chunks),
        out_shape=(
            jax.ShapeDtypeStruct((block, emb), jnp.float32),
            jax.ShapeDtypeStruct((1, rows), jnp.float32),
        ),
        in_specs=[VMEM] * 6,
        out_specs=(VMEM, VMEM),
        scratch_shapes=[
            f32(n_group, 2, emb), f32(n_dp, 2, emb), f32(2, emb),
            bf16(rows, emb), bf16(rows, emb), f32(rows, emb), f32(rows, emb), f32(rows, 1), f32(rows, 1),
            bf16(n_group, rows, emb), bf16(n_group, rows, emb), bf16(n_dp, rows, emb), bf16(n_dp, rows, emb),
            f32(n_dp, rows, rows),
            bf16(n_group, rows, rows), bf16(n_group, rows, rows), bf16(n_dp, rows, rows), bf16(n_dp, rows, rows),
            bf16(2, n_group, rows, depth), bf16(n_group, depth, 2 * rows), bf16(2, rows, emb),
            bf16(n_group, 2 * rows, emb),
            f32(chunks, n_dp, block, wide),
            bf16(chunks, max(1, inner - 1), line, block, wide),
            bf16(chunks, max(1, inner - 1), line, block, wide),
            bf16(chunks, line, block, wide), bf16(chunks, line, block, wide),
            f32(chunks, block, wide),
        ]
        + pairs(n_group) + pairs(n_dp) + pairs(2, n_group)
        + sems(2, 2, line) + sems(2, inner, line) + sems(2, n_dp) + pairs(2, n_group)
        + pairs(n_group) + pairs(n_dp)
        + pairs(2, chunks, n_group) + pairs(chunks, inner) + pairs(chunks, line)
        + ([bf16(2, n_group, rows, depth)] if inside else []),
        compiler_params=pltpu.CompilerParams(has_side_effects=True, vmem_limit_bytes=67043328),
        name="step",
    )(proj_query, proj_pass, stats, query_feats, pass_feats, named)


def body(query_feats, passage_feats, head, neg_ids):
    rows, width = query_feats.shape
    emb = head.shape[1]
    n_dp = lax.axis_size("dp")
    n_group = lax.axis_size("group")
    block = width // (n_dp * n_group)

    def cut(feats):
        if block % 128 == 0:
            return feats
        feats = feats.reshape(rows, n_dp, n_group, block)
        return feats.transpose(2, 0, 1, 3).reshape(n_group, rows, n_dp * block)

    proj_query = jnp.dot(query_feats, head, preferred_element_type=jnp.float32).astype(jnp.bfloat16)
    proj_pass = jnp.dot(passage_feats, head, preferred_element_type=jnp.float32).astype(
        jnp.bfloat16
    )
    col_high = jnp.maximum(jnp.max(proj_query, axis=0), jnp.max(proj_pass, axis=0)).astype(
        jnp.float32
    )
    col_low = jnp.minimum(jnp.min(proj_query, axis=0), jnp.min(proj_pass, axis=0)).astype(
        jnp.float32
    )
    named = (neg_ids // (n_group * rows)) * rows + neg_ids % rows
    head_grad, query_loss = whole_step(
        proj_query, proj_pass, jnp.stack([col_high, -col_low]), cut(query_feats),
        cut(passage_feats), named, n_dp, n_group, block,
    )
    return (head_grad, query_loss.reshape(rows))


def solution(mesh):
    return jax.shard_map(
        body,
        mesh=mesh,
        in_specs=(
            P(("dp", "group"), None),
            P(("dp", "group"), None),
            P(),
            P(("dp", "group"), None),
        ),
        out_specs=(P(("dp", "group"), None), P(("dp", "group"))),
        check_vma=False,
    )
```

profile of v0, /device:TPU:0, one launch (start us, length us, event | category | flops | bytes accessed | tf_op | source)
XLA Modules:
  0.0 126.7 jit_solution(12116769315665102307)
XLA Ops:
  0.6 0.0 copy-start
  0.6 0.9 copy.6
  1.5 0.0 slice-start
  1.5 0.7 fusion.2.named
  2.2 0.0 slice-start.1
  2.2 6.0 %fusion.6 = (bf16[1024]{0:T(1024)(128)(2,1)S(1)}, bf16[1024]{0:T(1024)(128)(2,1)S(1)}, bf16[128,1024]{1,0:T(8,128)(2,1)}) fusion(bf16[128,4096]{1,0:T(8,128)(2,1)} %query_feats.1, bf16[4096,1024]{1,0:T(8,128)(2,1)} %param.6), kind=kOutput, calls=%fused_computation.18 | convolution fusion | flops 1074132992 | bytes 9703424 | tf_op jit(solution)/shard_map/dot_general | solution.py:434
  8.2 0.0 copy-done
  8.2 0.0 slice-done
  8.2 0.0 slice-done.1
  8.2 2.0 %fusion.5 = (bf16[1024]{0:T(1024)(128)(2,1)S(1)}, bf16[1024]{0:T(1024)(128)(2,1)S(1)}, bf16[128,1024]{1,0:T(8,128)(2,1)}) fusion(bf16[128,4096]{1,0:T(8,128)(2,1)S(1)} %copy-done, bf16[4096,1024]{1,0:T(8,128)(2,1)S(1)} %bitcast.8), kind=kOutput, calls=%fused_computation.17 | convolution fusion | flops 1074132992 | bytes 9703424 | tf_op jit(solution)/shard_map/dot_general | solution.py:435
  10.3 0.6 pad_maximum_fusion.stats
  10.9 112.7 %step.1 = (f32[128,1024]{1,0:T(8,128)}, f32[1,128]{1,0:T(1,128)}) custom-call(bf16[128,1024]{1,0:T(8,128)(2,1)} %get-tuple-element.10.proj_query, bf16[128,1024]{1,0:T(8,128)(2,1)} %get-tuple-element.11.proj_pass, f32[2,1024]{1,0:T(2,128)} %pad_maximum_fusion.stats, bf16[128,4096]{1,0:T(8,128)(2,1)} %query_feats.1, bf16[128,4096]{1,0:T(8,128)(2,1)} %pass_feats.1, ...), custom_call_target="tpu_custom_call" | custom-call | tf_op jit(solution)/shard_map/step/pallas_call | solution.py:389
  123.6 1.9 %copy.12 = f32[128,1024]{1,0:T(8,128)} copy(f32[128,1024]{1,0:T(8,128)} %get-tuple-element.14) | data formatting | bytes 1048576
  125.5 1.2 copy.13
  (3 shorter events, 0.0 us)
Async XLA Ops:
  0.6 7.6 %copy-start = (bf16[128,4096]{1,0:T(8,128)(2,1)S(1)}, bf16[128,4096]{1,0:T(8,128)(2,1)}, u32[]{:S(2)}) copy-start(bf16[128,4096]{1,0:T(8,128)(2,1)} %pass_feats.1) | copy-start | bytes 3145732
  1.5 6.7 %slice-start = ((s8[8388608]{0:T(1024)(128)(4,1)}), s8[4194304]{0:T(1024)(128)(4,1)S(1)}, s32[]{:S(2)}) async-start(s8[8388608]{0:T(1024)(128)(4,1)} %bitcast.7), calls=%async_computation | async-start | bytes 8388608
  2.2 6.0 %slice-start.1 = ((s8[8388608]{0:T(1024)(128)(4,1)}), s8[4194304]{0:T(1024)(128)(4,1)S(1)}, s32[]{:S(2)}) async-start(s8[8388608]{0:T(1024)(128)(4,1)} %bitcast.7), calls=%async_computation.1 | async-start | bytes 8388608
where the time goes:
time: 128 us; the launch traced here: 127 us
  Pallas kernels  113 us (88%)
  matrix products  8.05 us (6%)
  local copies, waits for them, and re-layouts  3.95 us (3%)
  other arithmetic  1.29 us (1%)
    pallas_call x1, Pallas kernels, whole_step(): pl.pallas_call(functools.partial(step_kernel, n_dp, n_group, inner, chunk...  113 us
    dot_general x1, matrix products, body(): jnp.dot(query_feats, head, preferred_element_type=jnp.float32)  6.01 us
    unnamed x9, local copies, waits for them, and re-layouts  3.95 us

commit v1 on v0

--- a/solution.py
+++ b/solution.py
@@ -418,12 +418,433 @@
     )(proj_query, proj_pass, stats, query_feats, pass_feats, named)
 
 
+def chip_kernel(
+    n_dp, n_group, chunks, slabs,
+    pass_hbm, query_hbm, head_hbm, ids,
+    out, loss,
+    lhs, head, proj, stats, stats_dp, stats_mid, stats_group, ids_own, ids_in,
+    quant, inv, batch, dp_pass, dp_query, emb_dp,
+    exp_batch, hard_exp, batch_out, batch_in, row_out, row_in,
+    sent_feats, turned, dy, total, pair_out, pair_in, line_out, line_in, kept,
+    l_feat, l_head, l_own, s_stat_d, r_stat_d, s_stat_g, r_stat_g, s_ids, r_ids,
+    s_line, s_pair, r_dp, s_batch, r_batch, s_feat, r_feat, s_bw, r_bw, s_row, r_row,
+    s_dyq, r_dyq, s_dyp, r_dyp, s_p, r_p, s_l, r_l,
+):
+    me_d, me_g = lax.axis_index("dp"), lax.axis_index("group")
+    inner = 2
+    line = n_dp // inner
+    z, y = me_d // inner, lax.rem(me_d, inner)
+    chips = n_group // 2
+    chip, core = me_g // 2, lax.rem(me_g, 2)
+    rows, emb = proj.shape[1:]
+    wide = emb // chunks
+    slab = head.shape[0] // slabs
+    block = out.shape[0]
+    columns = lambda c: pl.ds(c * wide, wide)
+    own_rows = lambda g: pl.ds(pl.multiple_of(g * rows, rows), rows)
+    group_at = lambda k: lax.rem(me_g + k, n_group)
+    dp_at = lambda k: lax.rem(me_d + k, n_dp)
+    z_at = lambda k: lax.rem(z + k, line)
+    partner = chip * 2 + 1 - core
+    beside = [lax.rem(chip + j, chips) * 2 + core for j in range(1, chips)]
+    relayed = [lax.rem(chip + j, chips) * 2 + 1 - core for j in range(1, chips)]
+    others = [partner] + beside + relayed
+    across = z * inner + 1 - y
+
+    unsent = []
+
+    def send(src, dst, send_sem, recv_sem, device, condition=None):
+        copy = remote(src, dst, send_sem, recv_sem, device)
+        if condition is None:
+            copy.start()
+        else:
+            pl.when(condition)(copy.start)
+        unsent.append((condition, copy))
+
+    def arrived(dst, recv_sem):
+        remote(dst, dst, recv_sem, recv_sem, (me_d, partner)).wait_recv()
+
+    barrier = pltpu.get_barrier_semaphore()
+    peers = [(me_d, group_at(k)) for k in range(1, n_group)] + [(dp_at(k), me_g) for k in range(1, n_dp)]
+    for peer in peers:
+        pl.semaphore_signal(barrier, inc=1, device_id=peer, device_id_type=MESH)
+
+    loads = []
+    for i, source in enumerate((pass_hbm, query_hbm)):
+        loads.append(pltpu.make_async_copy(source, lhs.at[pl.ds(i * rows, rows)], l_feat.at[i]))
+    for s in range(slabs):
+        piece = pl.ds(s * slab, slab)
+        loads.append(pltpu.make_async_copy(head_hbm.at[piece], head.at[piece], l_head.at[s]))
+    for copy in loads:
+        copy.start()
+    ids_own[...] = jnp.full(ids_own.shape, -1, jnp.int32)
+    ids_own[0 : ids.shape[0]] = ids[...]
+    loads[0].wait()
+    loads[1].wait()
+    value = None
+    for s in range(slabs):
+        loads[2 + s].wait()
+        part = dot_nn(lhs[:, s * slab : (s + 1) * slab], head[s * slab : (s + 1) * slab])
+        value = part if value is None else value + part
+    rounded = value.astype(jnp.bfloat16)
+    proj[0] = rounded[:rows]
+    proj[1] = rounded[rows:]
+    seen = rounded.astype(jnp.float32)
+    stats[0:1] = jnp.max(seen, axis=0, keepdims=True)
+    stats[1:2] = -jnp.min(seen, axis=0, keepdims=True)
+    pl.semaphore_wait(barrier, len(peers))
+
+    for k in range(1, n_dp):
+        send(stats, stats_dp.at[k], s_stat_d.at[k], r_stat_d.at[k], (dp_at(k), me_g))
+
+    dp_bufs = (dp_pass, dp_query)
+
+    def along(i, at, src, rightward, leftward):
+        source = at * inner + y
+        dst = dp_bufs[i].at[source]
+        if rightward:
+            send(src, dst, s_line.at[i, 0, at], r_dp.at[i, source], (dp_at(inner), me_g), z < line - 1)
+        if leftward:
+            send(src, dst, s_line.at[i, 1, at], r_dp.at[i, source], (lax.rem(me_d + n_dp - inner, n_dp), me_g), z > 0)
+
+    def over(i, at, src):
+        source = at * inner + y
+        send(src, dp_bufs[i].at[source], s_pair.at[i, at], r_dp.at[i, source], (across, me_g))
+
+    relay_log = []
+
+    def relay(i, s):
+        for at, inside, onward in ((z - s, z >= s, 0), (z + s, z + s < line, 1)):
+            source = at * inner + y
+            block_ref = dp_bufs[i].at[source]
+            if onward == 0:
+                target, more = dp_at(inner), inside & (z < line - 1)
+            else:
+                target, more = lax.rem(me_d + n_dp - inner, n_dp), inside & (z > 0)
+            forward = remote(
+                block_ref, block_ref, s_line.at[i, onward, at], r_dp.at[i, source], (target, me_g)
+            )
+            side = remote(block_ref, block_ref, s_pair.at[i, at], r_dp.at[i, source], (across, me_g))
+
+            @pl.when(inside)
+            def _(block_ref=block_ref, source=source, side=side):
+                arrived(block_ref, r_dp.at[i, source])
+
+            pl.when(more)(forward.start)
+            pl.when(inside)(side.start)
+            unsent.append((more, forward))
+            unsent.append((inside, side))
+
+    along(0, z, proj.at[0], True, True)
+    over(0, z, proj.at[0])
+    for k in range(1, n_dp):
+        send(ids_own, ids_in.at[k], s_ids.at[k], r_ids.at[k], (dp_at(k), me_g))
+
+    bounds = stats[...]
+    for k in range(1, n_dp):
+        arrived(stats_dp.at[k], r_stat_d.at[k])
+        bounds = jnp.maximum(bounds, stats_dp[k])
+    stats_mid[...] = bounds
+    for k in range(1, n_group):
+        send(stats_mid, stats_group.at[k], s_stat_g.at[k], r_stat_g.at[k], (me_d, group_at(k)))
+    for k in range(1, n_group):
+        arrived(stats_group.at[k], r_stat_g.at[k])
+        bounds = jnp.maximum(bounds, stats_group[k])
+    high, low = bounds[0:1], -bounds[1:2]
+    stride = (high - low) / levels
+    inv_stride = 1.0 / stride
+
+    def embed(projected):
+        value = quantize(projected, low, stride, inv_stride)
+        inverse = lax.rsqrt(jnp.sum(value * value, axis=-1, keepdims=True) + epsilon)
+        return value, inverse, (value * inverse).astype(jnp.bfloat16)
+
+    for i in range(2):
+        quant[i], inv[i], batch[i, me_g] = embed(proj[i])
+        own = batch.at[i, me_g]
+        for m, target in enumerate([partner] + beside):
+            send(own, own, s_batch.at[i, m], r_batch.at[i, me_g], (me_d, target))
+
+    def hand_over(i):
+        for m, source in enumerate(beside):
+            landed = batch.at[i, source]
+            arrived(landed, r_batch.at[i, source])
+            send(landed, landed, s_batch.at[i, chips + m], r_batch.at[i, source], (me_d, partner))
+
+    relay(0, 1)
+    hand_over(0)
+
+    for i in (1, 0):
+        for d in range(n_dp * n_group):
+            sent_feats[i, d // n_group, d % n_group] = lhs[
+                i * rows : (i + 1) * rows, d * block : (d + 1) * block
+            ].T
+        for m, target in enumerate(others):
+            send(
+                sent_feats.at[i, :, target], turned.at[i, :, :, own_rows(me_g)],
+                s_feat.at[i, m], r_feat.at[i, me_g], (me_d, target),
+            )
+    stay = [
+        pltpu.make_async_copy(
+            sent_feats.at[i, :, me_g], turned.at[i, :, :, own_rows(me_g)], l_own.at[i]
+        )
+        for i in range(2)
+    ]
+    for copy in stay:
+        copy.start()
+
+    query = batch[1, me_g]
+    eye = (
+        lax.broadcasted_iota(jnp.int32, (rows, rows), 0)
+        == lax.broadcasted_iota(jnp.int32, (rows, rows), 1)
+    ).astype(jnp.float32)
+    place = lax.broadcasted_iota(jnp.int32, (rows, rows), 0)
+
+    def named(rows_of, device):
+        base = (device * n_group + me_g) * rows
+        here = rows_of[0:1] == place + base
+        for n in range(1, ids.shape[0]):
+            here = here | (rows_of[n : n + 1] == place + base)
+        return here
+
+    def hard_scores(source):
+        _, _, block_emb = embed(dp_pass[source])
+        emb_dp[source] = block_emb
+        score = dot_nt(block_emb, query) / scaling_divisor
+        hard_exp[source] = jnp.where(named(ids_own[...], source), jnp.exp(score), 0.0)
+
+    relay(0, 2) if line > 2 else None
+    along(1, z, batch.at[1, me_g], True, True)
+    arrived(dp_pass.at[across], r_dp.at[0, across])
+    hard_scores(across)
+    hand_over(1)
+    for s in range(3, line):
+        relay(0, s)
+    over(1, z, batch.at[1, me_g])
+
+    for source in [partner] + relayed:
+        arrived(batch.at[0, source], r_batch.at[0, source])
+    own_score = dot_nt(batch[0, me_g], query) / scaling_divisor
+    positive = jnp.sum(own_score * eye, axis=0, keepdims=True)
+    own_exp = jnp.exp(own_score)
+    batch_total = jnp.sum(own_exp, axis=0, keepdims=True)
+    for m, source in enumerate(others):
+        weight = jnp.exp(dot_nt(batch[0, source], query) / scaling_divisor)
+        exp_batch[m] = weight
+        batch_total += jnp.sum(weight, axis=0, keepdims=True)
+    exp_pos = jnp.exp(positive)
+
+    for k in range(1, line):
+        hard_scores(z_at(k) * inner + y)
+        if k == 1:
+            relay(1, 1)
+    for k in range(1, line):
+        source = z_at(k) * inner + 1 - y
+        arrived(dp_pass.at[source], r_dp.at[0, source])
+        hard_scores(source)
+
+    hard_sum = hard_exp[dp_at(1)]
+    for k in range(2, n_dp):
+        hard_sum += hard_exp[dp_at(k)]
+    hard_total = exp_pos + jnp.sum(hard_sum, axis=0, keepdims=True)
+    loss[...] = jnp.log(batch_total) - positive + jnp.log(hard_total) - positive
+
+    for m, target in enumerate(others):
+        batch_out[target] = (exp_batch[m] / batch_total).astype(jnp.bfloat16)
+        send(batch_out.at[target], batch_in.at[me_g], s_bw.at[m], r_bw.at[me_g], (me_d, target))
+    own_weight = (own_exp / batch_total - eye * (2.0 - exp_pos / hard_total)).astype(jnp.bfloat16)
+    grad = dot_tn(own_weight, batch[0, me_g])
+    for source in others:
+        grad += dot_tn(batch_out[source], batch[0, source])
+    for k in range(1, n_dp):
+        source = dp_at(k)
+        weight = (hard_exp[source] / hard_total).astype(jnp.bfloat16)
+        row = jnp.sum(weight.astype(jnp.float32), axis=0, keepdims=True)
+        row_out[k] = jnp.broadcast_to(row, row_out.shape[1:])
+        send(row_out.at[k], row_in.at[k], s_row.at[k], r_row.at[k], (source, me_g))
+        grad += dot_tn(weight, emb_dp[source])
+    if line > 2:
+        relay(1, 2)
+    dy[1, own_rows(me_g)] = norm_back(grad / scaling_divisor, quant[1], inv[1])
+    own = dy.at[1, own_rows(me_g)]
+    for m, target in enumerate([partner] + beside):
+        send(own, own, s_dyq.at[m], r_dyq.at[me_g], (me_d, target))
+
+    for source in [partner] + relayed:
+        arrived(batch.at[1, source], r_batch.at[1, source])
+    grad = dot_nn(own_weight, query)
+    for source in others:
+        arrived(batch_in.at[source], r_bw.at[source])
+        grad += dot_nn(batch_in[source], batch[1, source])
+    grad = grad / scaling_divisor
+
+    for m, source in enumerate(beside):
+        landed = dy.at[1, own_rows(source)]
+        arrived(landed, r_dyq.at[source])
+        send(landed, landed, s_dyq.at[chips + m], r_dyq.at[source], (me_d, partner))
+    for k in range(1, n_dp):
+        arrived(ids_in.at[k], r_ids.at[k])
+        arrived(row_in.at[k], r_row.at[k])
+
+    def hard_back(source, k):
+        weight = jnp.sum(row_in[k][0:1] * eye, axis=1, keepdims=True)
+        hard = (weight * dp_query[source].astype(jnp.float32) * (1.0 / scaling_divisor)).astype(
+            jnp.bfloat16
+        )
+        chosen = jnp.where(named(ids_in[k], me_d), 1.0, 0.0).astype(jnp.bfloat16)
+        return dot_nn(chosen, hard)
+
+    def behind(source):
+        return lax.rem(me_d + n_dp - source, n_dp)
+
+    arrived(dp_query.at[across], r_dp.at[1, across])
+    grad += hard_back(across, behind(across))
+
+    for copy in stay:
+        copy.wait()
+    for source in others:
+        arrived(turned.at[1, :, :, own_rows(source)], r_feat.at[1, source])
+    for source in [partner] + relayed:
+        arrived(dy.at[1, own_rows(source)], r_dyq.at[source])
+    depth = n_dp * block
+    seen_rows = lambda i: turned[i].reshape(depth, n_group * rows)
+    for c in range(chunks):
+        total[c] = dot_nn(seen_rows(1), dy[1, :, columns(c)]).reshape(n_dp, block, wide)
+        if c == 1:
+            for s in range(3, line):
+                relay(1, s)
+    for source in others:
+        arrived(turned.at[0, :, :, own_rows(source)], r_feat.at[0, source])
+    for k in range(1, line):
+        source = z_at(k) * inner + y
+        grad += hard_back(source, behind(source))
+    for k in range(1, line):
+        source = z_at(k) * inner + 1 - y
+        arrived(dp_query.at[source], r_dp.at[1, source])
+        grad += hard_back(source, behind(source))
+
+    dy[0, own_rows(me_g)] = norm_back(grad, quant[0], inv[0])
+    for c in range(chunks):
+        own = dy.at[0, own_rows(me_g), columns(c)]
+        for m, target in enumerate(beside):
+            send(own, own, s_dyp.at[c, 1 + m], r_dyp.at[c, me_g], (me_d, target))
+        send(own, own, s_dyp.at[c, 0], r_dyp.at[c, me_g], (me_d, partner))
+
+    def pass_on(c):
+        for m, source in enumerate(beside):
+            landed = dy.at[0, own_rows(source), columns(c)]
+            arrived(landed, r_dyp.at[c, source])
+            send(landed, landed, s_dyp.at[c, chips + m], r_dyp.at[c, source], (me_d, partner))
+
+    def first(c):
+        for source in [partner] + relayed:
+            arrived(dy.at[0, own_rows(source), columns(c)], r_dyp.at[c, source])
+        part = dot_nn(seen_rows(0), dy[0, :, columns(c)]).reshape(n_dp, block, wide)
+        total[c] += part
+        for at in range(line):
+            pair_out[c, at] = total[c, at * inner + 1 - y].astype(jnp.bfloat16)
+        send(pair_out.at[c], pair_in.at[c], s_p.at[c], r_p.at[c], (across, me_g))
+
+    def second(c):
+        arrived(pair_in.at[c], r_p.at[c])
+        summed = lambda at: total[c, at * inner + y] + pair_in[c, at].astype(jnp.float32)
+        for j in range(1, line):
+            line_out[c, j] = summed(z_at(j)).astype(jnp.bfloat16)
+            send(
+                line_out.at[c, j], line_in.at[c, j], s_l.at[c, j], r_l.at[c, j],
+                (z_at(j) * inner + y, me_g),
+            )
+        kept[c] = summed(z)
+
+    def third(c):
+        value = kept[c]
+        for j in range(1, line):
+            arrived(line_in.at[c, j], r_l.at[c, j])
+            value += line_in[c, j].astype(jnp.float32)
+        out[:, columns(c)] = value
+
+    lag = 3
+    pass_on(0)
+    for c in range(chunks):
+        if c + 1 < chunks:
+            pass_on(c + 1)
+        first(c)
+        if c >= lag:
+            second(c - lag)
+    for c in range(max(0, chunks - lag), chunks):
+        second(c)
+    for c in range(chunks):
+        third(c)
+    for condition, copy in unsent:
+        if condition is None:
+            copy.wait_send()
+        else:
+            pl.when(condition)(copy.wait_send)
+
+
+def chip_step(pass_feats, query_feats, head, ids, n_dp, n_group, block):
+    rows, width = pass_feats.shape
+    emb = head.shape[1]
+    line, chips = n_dp // 2, n_group // 2
+    chunks = emb // 128
+    slabs = max(1, width // 512)
+    wide = emb // chunks
+    bf16 = lambda *shape: pltpu.VMEM(shape, jnp.bfloat16)
+    f32 = lambda *shape: pltpu.VMEM(shape, jnp.float32)
+    i32 = lambda *shape: pltpu.VMEM(shape, jnp.int32)
+    sems = lambda *shape: [pltpu.SemaphoreType.DMA(shape)]
+    pairs = lambda *shape: sems(*shape) * 2
+    anywhere = pl.BlockSpec(memory_space=pl.ANY)
+    return pl.pallas_call(
+        functools.partial(chip_kernel, n_dp, n_group, chunks, slabs),
+        out_shape=(
+            jax.ShapeDtypeStruct((block, emb), jnp.float32),
+            jax.ShapeDtypeStruct((1, rows), jnp.float32),
+        ),
+        in_specs=[anywhere, anywhere, anywhere, VMEM],
+        out_specs=(VMEM, VMEM),
+        scratch_shapes=[
+            bf16(2 * rows, width), bf16(width, emb), bf16(2, rows, emb),
+            f32(2, emb), f32(n_dp, 2, emb), f32(2, emb), f32(n_group, 2, emb),
+            i32(8, rows), i32(n_dp, 8, rows),
+            f32(2, rows, emb), f32(2, rows, 1), bf16(2, n_group, rows, emb),
+            bf16(n_dp, rows, emb), bf16(n_dp, rows, emb), bf16(n_dp, rows, emb),
+            f32(n_group, rows, rows), f32(n_dp, rows, rows),
+            bf16(n_group, rows, rows), bf16(n_group, rows, rows),
+            f32(n_dp, 8, rows), f32(n_dp, 8, rows),
+            bf16(2, n_dp, n_group, block, rows), bf16(2, n_dp, block, n_group * rows),
+            bf16(2, n_group * rows, emb),
+            f32(chunks, n_dp, block, wide),
+            bf16(chunks, line, block, wide), bf16(chunks, line, block, wide),
+            bf16(chunks, line, block, wide), bf16(chunks, line, block, wide),
+            f32(chunks, block, wide),
+        ]
+        + sems(2) + sems(slabs) + sems(2) + pairs(n_dp) + pairs(n_group) + pairs(n_dp)
+        + sems(2, 2, line) + sems(2, line) + sems(2, n_dp)
+        + sems(2, 2 * chips) + sems(2, n_group)
+        + sems(2, n_group) + sems(2, n_group)
+        + pairs(n_group) + pairs(n_dp)
+        + sems(2 * chips) + sems(n_group)
+        + sems(chunks, 2 * chips) + sems(chunks, n_group)
+        + pairs(chunks) + pairs(chunks, line),
+        compiler_params=pltpu.CompilerParams(
+            has_side_effects=True, collective_id=0, vmem_limit_bytes=60 * 2**20
+        ),
+        name="chip_step",
+    )(pass_feats, query_feats, head, ids)
+
+
 def body(query_feats, passage_feats, head, neg_ids):
     rows, width = query_feats.shape
     emb = head.shape[1]
     n_dp = lax.axis_size("dp")
     n_group = lax.axis_size("group")
     block = width // (n_dp * n_group)
+    if n_dp <= 16 and n_dp % 2 == 0 and n_group % 2 == 0 and block % 128 == 0:
+        head_grad, query_loss = chip_step(
+            passage_feats, query_feats, head, neg_ids.T, n_dp, n_group, block
+        )
+        return (head_grad, query_loss.reshape(rows))
 
     def cut(feats):
         if block % 128 == 0:

time: 128 us -> 113 us (0.88)
  matrix products: 8.05 us -> 0 us
  Pallas kernels: 113 us -> 109 us
  other arithmetic: 1.29 us -> 0 us
    dot_general x2 -> x0, matrix products: 8.05 us -> none  [the longest x1 6.01 us: body(): jnp.dot(query_feats, head, preferred_element_type=jnp.float32)]
    pallas_call x1, Pallas kernels: 113 us -> 109 us  [chip_step(): pl.pallas_call(functools.partial(chip_kernel, n_dp, n_group, chunks, slab...]
    unnamed x9 -> x2, local copies, waits for them, and re-layouts: 3.95 us -> 2.99 us
where the time goes in v1:
time: 113 us
  Pallas kernels  109 us (96%)
  local copies, waits for them, and re-layouts  2.99 us (3%)
    pallas_call x1, Pallas kernels, chip_step(): pl.pallas_call(functools.partial(chip_kernel, n_dp, n_group, chunks, slab...  109 us
    unnamed x2, local copies, waits for them, and re-layouts  2.99 us

profile of v1, /device:TPU:0, one launch (start us, length us, event | category | flops | bytes accessed | tf_op | source)
XLA Modules:
  0.0 112.6 jit_solution(13667618884223236226)
XLA Ops:
  0.6 108.9 %chip_step.1 = (f32[128,1024]{1,0:T(8,128)}, f32[1,128]{1,0:T(1,128)}) custom-call(bf16[128,4096]{1,0:T(8,128)(2,1)} %pass_hbm.1, bf16[128,4096]{1,0:T(8,128)(2,1)} %query_hbm.1, bf16[4096,1024]{1,0:T(8,128)(2,1)} %head_hbm.1, s32[7,128]{1,0:T(8,128)} %bitcast.2), custom_call_target="tpu_custom_call" | custom-call | tf_op jit(solution)/shard_map/chip_step/pallas_call | solution.py:798
  109.6 1.9 %copy.8 = f32[128,1024]{1,0:T(8,128)} copy(f32[128,1024]{1,0:T(8,128)} %get-tuple-element.8) | data formatting | bytes 1048576
  111.5 1.1 copy.9

commit v2 on v1

--- a/solution.py
+++ b/solution.py
@@ -427,7 +427,7 @@
     exp_batch, hard_exp, batch_out, batch_in, row_out, row_in,
     sent_feats, turned, dy, total, pair_out, pair_in, line_out, line_in, kept,
     l_feat, l_head, l_own, s_stat_d, r_stat_d, s_stat_g, r_stat_g, s_ids, r_ids,
-    s_line, s_pair, r_dp, s_batch, r_batch, s_feat, r_feat, s_bw, r_bw, s_row, r_row,
+    s_line, s_pair, r_dp, s_half, r_half, s_batch, r_batch, s_feat, r_feat, s_bw, r_bw, s_row, r_row,
     s_dyq, r_dyq, s_dyp, r_dyp, s_p, r_p, s_l, r_l,
 ):
     me_d, me_g = lax.axis_index("dp"), lax.axis_index("group")
@@ -438,13 +438,23 @@
     chip, core = me_g // 2, lax.rem(me_g, 2)
     rows, emb = proj.shape[1:]
     wide = emb // chunks
-    slab = head.shape[0] // slabs
+    slab = emb // slabs
     block = out.shape[0]
     columns = lambda c: pl.ds(c * wide, wide)
     own_rows = lambda g: pl.ds(pl.multiple_of(g * rows, rows), rows)
     group_at = lambda k: lax.rem(me_g + k, n_group)
     dp_at = lambda k: lax.rem(me_d + k, n_dp)
+    dp_from = lambda k: lax.rem(me_d + n_dp - k, n_dp)
     z_at = lambda k: lax.rem(z + k, line)
+
+    def plane(k):
+        value = z
+        for bit in range(k.bit_length()):
+            if k >> bit & 1:
+                value = value + (1 - 2 * lax.rem(z // (1 << bit), 2)) * (1 << bit)
+        return value
+
+    half = rows // 2
     partner = chip * 2 + 1 - core
     beside = [lax.rem(chip + j, chips) * 2 + core for j in range(1, chips)]
     relayed = [lax.rem(chip + j, chips) * 2 + 1 - core for j in range(1, chips)]
@@ -474,24 +484,24 @@
         loads.append(pltpu.make_async_copy(source, lhs.at[pl.ds(i * rows, rows)], l_feat.at[i]))
     for s in range(slabs):
         piece = pl.ds(s * slab, slab)
-        loads.append(pltpu.make_async_copy(head_hbm.at[piece], head.at[piece], l_head.at[s]))
+        loads.append(
+            pltpu.make_async_copy(head_hbm.at[:, piece], head.at[:, piece], l_head.at[s])
+        )
     for copy in loads:
         copy.start()
     ids_own[...] = jnp.full(ids_own.shape, -1, jnp.int32)
     ids_own[0 : ids.shape[0]] = ids[...]
     loads[0].wait()
     loads[1].wait()
-    value = None
     for s in range(slabs):
         loads[2 + s].wait()
-        part = dot_nn(lhs[:, s * slab : (s + 1) * slab], head[s * slab : (s + 1) * slab])
-        value = part if value is None else value + part
-    rounded = value.astype(jnp.bfloat16)
-    proj[0] = rounded[:rows]
-    proj[1] = rounded[rows:]
-    seen = rounded.astype(jnp.float32)
-    stats[0:1] = jnp.max(seen, axis=0, keepdims=True)
-    stats[1:2] = -jnp.min(seen, axis=0, keepdims=True)
+        piece = slice(s * slab, (s + 1) * slab)
+        rounded = dot_nn(lhs[...], head[:, piece]).astype(jnp.bfloat16)
+        proj[0, :, piece] = rounded[:rows]
+        proj[1, :, piece] = rounded[rows:]
+        seen = rounded.astype(jnp.float32)
+        stats[0:1, piece] = jnp.max(seen, axis=0, keepdims=True)
+        stats[1:2, piece] = -jnp.min(seen, axis=0, keepdims=True)
     pl.semaphore_wait(barrier, len(peers))
 
     for k in range(1, n_dp):
@@ -505,41 +515,75 @@
         if rightward:
             send(src, dst, s_line.at[i, 0, at], r_dp.at[i, source], (dp_at(inner), me_g), z < line - 1)
         if leftward:
-            send(src, dst, s_line.at[i, 1, at], r_dp.at[i, source], (lax.rem(me_d + n_dp - inner, n_dp), me_g), z > 0)
+            send(src, dst, s_line.at[i, 1, at], r_dp.at[i, source], (dp_from(inner), me_g), z > 0)
 
     def over(i, at, src):
         source = at * inner + y
         send(src, dp_bufs[i].at[source], s_pair.at[i, at], r_dp.at[i, source], (across, me_g))
 
-    relay_log = []
-
     def relay(i, s):
         for at, inside, onward in ((z - s, z >= s, 0), (z + s, z + s < line, 1)):
             source = at * inner + y
-            block_ref = dp_bufs[i].at[source]
+            landed = dp_bufs[i].at[source]
+            part = landed.at[pl.ds(0, half)]
             if onward == 0:
-                target, more = dp_at(inner), inside & (z < line - 1)
+                target, more, twin = dp_at(inner), inside & (z < line - 1), lax.rem(z, 2) == 1
             else:
-                target, more = lax.rem(me_d + n_dp - inner, n_dp), inside & (z > 0)
-            forward = remote(
-                block_ref, block_ref, s_line.at[i, onward, at], r_dp.at[i, source], (target, me_g)
-            )
-            side = remote(block_ref, block_ref, s_pair.at[i, at], r_dp.at[i, source], (across, me_g))
+                target, more, twin = dp_from(inner), inside & (z > 0), lax.rem(z, 2) == 0
+            recv = r_dp.at[i, source]
+            steps = [(more, remote(landed, landed, s_line.at[i, onward, at], recv, (target, me_g)))]
+            side = remote(landed, landed, s_pair.at[i, at], recv, (across, me_g))
+            if s == 1:
+                steps.append((inside & jnp.logical_not(twin), side))
+                steps.append(
+                    (inside & twin, remote(part, part, s_pair.at[i, at], recv, (across, me_g)))
+                )
+            else:
+                steps.append((inside, side))
 
             @pl.when(inside)
-            def _(block_ref=block_ref, source=source, side=side):
-                arrived(block_ref, r_dp.at[i, source])
-
-            pl.when(more)(forward.start)
-            pl.when(inside)(side.start)
-            unsent.append((more, forward))
-            unsent.append((inside, side))
+            def _(landed=landed, recv=recv):
+                arrived(landed, recv)
+
+            for condition, copy in steps:
+                pl.when(condition)(copy.start)
+                unsent.append((condition, copy))
+
+    def lower(i):
+        arrived(dp_bufs[i].at[across], r_dp.at[i, across])
+        part = dp_bufs[i].at[across, pl.ds(half, half)]
+        send(part, part, s_half.at[i], r_half.at[i], (plane(1) * inner + y, me_g))
+
+    def gathered(i, k):
+        source = plane(k) * inner + 1 - y
+        landed = dp_bufs[i].at[source]
+        if k == 1:
+            arrived(landed.at[pl.ds(0, half)], r_dp.at[i, source])
+            arrived(landed.at[pl.ds(half, half)], r_half.at[i])
+        else:
+            arrived(landed, r_dp.at[i, source])
+        return source
+
+    def turn(i):
+        for d in range(n_dp * n_group):
+            sent_feats[i, d // n_group, d % n_group] = lhs[
+                i * rows : (i + 1) * rows, d * block : (d + 1) * block
+            ].T
+
+    def send_feats(i, which):
+        for m, target in enumerate(others):
+            if m in which:
+                send(
+                    sent_feats.at[i, :, target], turned.at[i, :, :, own_rows(me_g)],
+                    s_feat.at[i, m], r_feat.at[i, me_g], (me_d, target),
+                )
 
     along(0, z, proj.at[0], True, True)
     over(0, z, proj.at[0])
     for k in range(1, n_dp):
         send(ids_own, ids_in.at[k], s_ids.at[k], r_ids.at[k], (dp_at(k), me_g))
 
+    turn(1)
     bounds = stats[...]
     for k in range(1, n_dp):
         arrived(stats_dp.at[k], r_stat_d.at[k])
@@ -547,6 +591,9 @@
     stats_mid[...] = bounds
     for k in range(1, n_group):
         send(stats_mid, stats_group.at[k], s_stat_g.at[k], r_stat_g.at[k], (me_d, group_at(k)))
+    send_feats(1, range(chips))
+    relay(0, 1)
+    lower(0)
     for k in range(1, n_group):
         arrived(stats_group.at[k], r_stat_g.at[k])
         bounds = jnp.maximum(bounds, stats_group[k])
@@ -571,19 +618,8 @@
             arrived(landed, r_batch.at[i, source])
             send(landed, landed, s_batch.at[i, chips + m], r_batch.at[i, source], (me_d, partner))
 
-    relay(0, 1)
-    hand_over(0)
-
-    for i in (1, 0):
-        for d in range(n_dp * n_group):
-            sent_feats[i, d // n_group, d % n_group] = lhs[
-                i * rows : (i + 1) * rows, d * block : (d + 1) * block
-            ].T
-        for m, target in enumerate(others):
-            send(
-                sent_feats.at[i, :, target], turned.at[i, :, :, own_rows(me_g)],
-                s_feat.at[i, m], r_feat.at[i, me_g], (me_d, target),
-            )
+    send_feats(1, range(chips, n_group))
+    turn(0)
     stay = [
         pltpu.make_async_copy(
             sent_feats.at[i, :, me_g], turned.at[i, :, :, own_rows(me_g)], l_own.at[i]
@@ -613,14 +649,16 @@
         score = dot_nt(block_emb, query) / scaling_divisor
         hard_exp[source] = jnp.where(named(ids_own[...], source), jnp.exp(score), 0.0)
 
-    relay(0, 2) if line > 2 else None
+    hard_scores(across)
+    if line > 2:
+        relay(0, 2)
     along(1, z, batch.at[1, me_g], True, True)
-    arrived(dp_pass.at[across], r_dp.at[0, across])
-    hard_scores(across)
-    hand_over(1)
+    hand_over(0)
+    send_feats(0, range(chips))
     for s in range(3, line):
         relay(0, s)
     over(1, z, batch.at[1, me_g])
+    hand_over(1)
 
     for source in [partner] + relayed:
         arrived(batch.at[0, source], r_batch.at[0, source])
@@ -635,13 +673,11 @@
     exp_pos = jnp.exp(positive)
 
     for k in range(1, line):
-        hard_scores(z_at(k) * inner + y)
-        if k == 1:
-            relay(1, 1)
+        hard_scores(plane(k) * inner + y)
+    relay(1, 1)
+    lower(1)
     for k in range(1, line):
-        source = z_at(k) * inner + 1 - y
-        arrived(dp_pass.at[source], r_dp.at[0, source])
-        hard_scores(source)
+        hard_scores(gathered(0, k))
 
     hard_sum = hard_exp[dp_at(1)]
     for k in range(2, n_dp):
@@ -663,12 +699,13 @@
         row_out[k] = jnp.broadcast_to(row, row_out.shape[1:])
         send(row_out.at[k], row_in.at[k], s_row.at[k], r_row.at[k], (source, me_g))
         grad += dot_tn(weight, emb_dp[source])
-    if line > 2:
-        relay(1, 2)
     dy[1, own_rows(me_g)] = norm_back(grad / scaling_divisor, quant[1], inv[1])
     own = dy.at[1, own_rows(me_g)]
     for m, target in enumerate([partner] + beside):
         send(own, own, s_dyq.at[m], r_dyq.at[me_g], (me_d, target))
+    send_feats(0, range(chips, n_group))
+    if line > 2:
+        relay(1, 2)
 
     for source in [partner] + relayed:
         arrived(batch.at[1, source], r_batch.at[1, source])
@@ -677,29 +714,28 @@
         arrived(batch_in.at[source], r_bw.at[source])
         grad += dot_nn(batch_in[source], batch[1, source])
     grad = grad / scaling_divisor
-
+    for k in range(1, n_dp):
+        arrived(ids_in.at[k], r_ids.at[k])
+
+    def hard_back(source):
+        k = lax.rem(me_d + n_dp - source, n_dp)
+        arrived(row_in.at[k], r_row.at[k])
+        weight = jnp.sum(row_in[k][0:1] * eye, axis=1, keepdims=True)
+        hard = (weight * dp_query[source].astype(jnp.float32) * (1.0 / scaling_divisor)).astype(
+            jnp.bfloat16
+        )
+        chosen = jnp.where(named(ids_in[k], me_d), 1.0, 0.0).astype(jnp.bfloat16)
+        return dot_nn(chosen, hard)
+
+    grad += hard_back(across)
+    for s in range(3, line):
+        relay(1, s)
     for m, source in enumerate(beside):
         landed = dy.at[1, own_rows(source)]
         arrived(landed, r_dyq.at[source])
         send(landed, landed, s_dyq.at[chips + m], r_dyq.at[source], (me_d, partner))
-    for k in range(1, n_dp):
-        arrived(ids_in.at[k], r_ids.at[k])
-        arrived(row_in.at[k], r_row.at[k])
-
-    def hard_back(source, k):
-        weight = jnp.sum(row_in[k][0:1] * eye, axis=1, keepdims=True)
-        hard = (weight * dp_query[source].astype(jnp.float32) * (1.0 / scaling_divisor)).astype(
-            jnp.bfloat16
-        )
-        chosen = jnp.where(named(ids_in[k], me_d), 1.0, 0.0).astype(jnp.bfloat16)
-        return dot_nn(chosen, hard)
-
-    def behind(source):
-        return lax.rem(me_d + n_dp - source, n_dp)
-
-    arrived(dp_query.at[across], r_dp.at[1, across])
-    grad += hard_back(across, behind(across))
-
+    for k in range(1, line):
+        grad += hard_back(plane(k) * inner + y)
     for copy in stay:
         copy.wait()
     for source in others:
@@ -708,20 +744,12 @@
         arrived(dy.at[1, own_rows(source)], r_dyq.at[source])
     depth = n_dp * block
     seen_rows = lambda i: turned[i].reshape(depth, n_group * rows)
-    for c in range(chunks):
-        total[c] = dot_nn(seen_rows(1), dy[1, :, columns(c)]).reshape(n_dp, block, wide)
-        if c == 1:
-            for s in range(3, line):
-                relay(1, s)
-    for source in others:
-        arrived(turned.at[0, :, :, own_rows(source)], r_feat.at[0, source])
+    from_query = lambda c: dot_nn(seen_rows(1), dy[1, :, columns(c)]).reshape(n_dp, block, wide)
+    early = min(2, chunks)
+    for c in range(early):
+        total[c] = from_query(c)
     for k in range(1, line):
-        source = z_at(k) * inner + y
-        grad += hard_back(source, behind(source))
-    for k in range(1, line):
-        source = z_at(k) * inner + 1 - y
-        arrived(dp_query.at[source], r_dp.at[1, source])
-        grad += hard_back(source, behind(source))
+        grad += hard_back(gathered(1, k))
 
     dy[0, own_rows(me_g)] = norm_back(grad, quant[0], inv[0])
     for c in range(chunks):
@@ -740,7 +768,7 @@
         for source in [partner] + relayed:
             arrived(dy.at[0, own_rows(source), columns(c)], r_dyp.at[c, source])
         part = dot_nn(seen_rows(0), dy[0, :, columns(c)]).reshape(n_dp, block, wide)
-        total[c] += part
+        total[c] = part + (total[c] if c < early else from_query(c))
         for at in range(line):
             pair_out[c, at] = total[c, at * inner + 1 - y].astype(jnp.bfloat16)
         send(pair_out.at[c], pair_in.at[c], s_p.at[c], r_p.at[c], (across, me_g))
@@ -764,6 +792,8 @@
         out[:, columns(c)] = value
 
     lag = 3
+    for source in others:
+        arrived(turned.at[0, :, :, own_rows(source)], r_feat.at[0, source])
     pass_on(0)
     for c in range(chunks):
         if c + 1 < chunks:
@@ -787,7 +817,7 @@
     emb = head.shape[1]
     line, chips = n_dp // 2, n_group // 2
     chunks = emb // 128
-    slabs = max(1, width // 512)
+    slabs = max(1, emb // 256)
     wide = emb // chunks
     bf16 = lambda *shape: pltpu.VMEM(shape, jnp.bfloat16)
     f32 = lambda *shape: pltpu.VMEM(shape, jnp.float32)
@@ -820,7 +850,7 @@
             f32(chunks, block, wide),
         ]
         + sems(2) + sems(slabs) + sems(2) + pairs(n_dp) + pairs(n_group) + pairs(n_dp)
-        + sems(2, 2, line) + sems(2, line) + sems(2, n_dp)
+        + sems(2, 2, line) + sems(2, line) + sems(2, n_dp) + pairs(2)
         + sems(2, 2 * chips) + sems(2, n_group)
         + sems(2, n_group) + sems(2, n_group)
         + pairs(n_group) + pairs(n_dp)

time: 113 us -> 107 us (0.947)
  Pallas kernels: 109 us -> 103 us
    pallas_call x1, Pallas kernels: 109 us -> 103 us  [chip_step(): pl.pallas_call(functools.partial(chip_kernel, n_dp, n_group, chunks, slab...]
where the time goes in v2:
time: 107 us
  Pallas kernels  103 us (96%)
  local copies, waits for them, and re-layouts  2.99 us (3%)
    pallas_call x1, Pallas kernels, chip_step(): pl.pallas_call(functools.partial(chip_kernel, n_dp, n_group, chunks, slab...  103 us
    unnamed x2, local copies, waits for them, and re-layouts  2.99 us

profile of v2, /device:TPU:0, one launch (start us, length us, event | category | flops | bytes accessed | tf_op | source)
XLA Modules:
  0.0 106.6 jit_solution(2513910130929698433)
XLA Ops:
  0.6 102.9 %chip_step.1 = (f32[128,1024]{1,0:T(8,128)}, f32[1,128]{1,0:T(1,128)}) custom-call(bf16[128,4096]{1,0:T(8,128)(2,1)} %pass_hbm.1, bf16[128,4096]{1,0:T(8,128)(2,1)} %query_hbm.1, bf16[4096,1024]{1,0:T(8,128)(2,1)} %head_hbm.1, s32[7,128]{1,0:T(8,128)} %bitcast.2), custom_call_target="tpu_custom_call" | custom-call | tf_op jit(solution)/shard_map/chip_step/pallas_call | solution.py:828
  103.6 1.9 %copy.8 = f32[128,1024]{1,0:T(8,128)} copy(f32[128,1024]{1,0:T(8,128)} %get-tuple-element.8) | data formatting | bytes 1048576
  105.4 1.1 %copy.9 = f32[128]{0:T(128)} copy(f32[128]{0:T(128)} %bitcast.3) | data formatting | bytes 1024

commit v3 on v2

--- a/solution.py
+++ b/solution.py
@@ -422,11 +422,11 @@
     n_dp, n_group, chunks, slabs,
     pass_hbm, query_hbm, head_hbm, ids,
     out, loss,
-    lhs, head, proj, stats, stats_dp, stats_mid, stats_group, ids_own, ids_in,
+    lhs, head, acc, proj, stats, stats_dp, stats_mid, stats_group, ids_own, ids_in,
     quant, inv, batch, dp_pass, dp_query, emb_dp,
     exp_batch, hard_exp, batch_out, batch_in, row_out, row_in,
     sent_feats, turned, dy, total, pair_out, pair_in, line_out, line_in, kept,
-    l_feat, l_head, l_own, s_stat_d, r_stat_d, s_stat_g, r_stat_g, s_ids, r_ids,
+    l_feat, l_head, l_own, l_out, s_stat_d, r_stat_d, s_stat_g, r_stat_g, s_ids, r_ids,
     s_line, s_pair, r_dp, s_half, r_half, s_batch, r_batch, s_feat, r_feat, s_bw, r_bw, s_row, r_row,
     s_dyq, r_dyq, s_dyp, r_dyp, s_p, r_p, s_l, r_l,
 ):
@@ -438,7 +438,7 @@
     chip, core = me_g // 2, lax.rem(me_g, 2)
     rows, emb = proj.shape[1:]
     wide = emb // chunks
-    slab = emb // slabs
+    slab = head.shape[0] // slabs
     block = out.shape[0]
     columns = lambda c: pl.ds(c * wide, wide)
     own_rows = lambda g: pl.ds(pl.multiple_of(g * rows, rows), rows)
@@ -480,28 +480,39 @@
         pl.semaphore_signal(barrier, inc=1, device_id=peer, device_id_type=MESH)
 
     loads = []
-    for i, source in enumerate((pass_hbm, query_hbm)):
-        loads.append(pltpu.make_async_copy(source, lhs.at[pl.ds(i * rows, rows)], l_feat.at[i]))
     for s in range(slabs):
         piece = pl.ds(s * slab, slab)
-        loads.append(
-            pltpu.make_async_copy(head_hbm.at[:, piece], head.at[:, piece], l_head.at[s])
-        )
+        for i, source in enumerate((pass_hbm, query_hbm)):
+            loads.append(
+                pltpu.make_async_copy(
+                    source.at[:, piece], lhs.at[pl.ds(i * rows, rows), piece], l_feat.at[i, s]
+                )
+            )
+        loads.append(pltpu.make_async_copy(head_hbm.at[piece], head.at[piece], l_head.at[s]))
     for copy in loads:
         copy.start()
     ids_own[...] = jnp.full(ids_own.shape, -1, jnp.int32)
     ids_own[0 : ids.shape[0]] = ids[...]
-    loads[0].wait()
-    loads[1].wait()
     for s in range(slabs):
-        loads[2 + s].wait()
+        for copy in loads[3 * s : 3 * s + 3]:
+            copy.wait()
         piece = slice(s * slab, (s + 1) * slab)
-        rounded = dot_nn(lhs[...], head[:, piece]).astype(jnp.bfloat16)
-        proj[0, :, piece] = rounded[:rows]
-        proj[1, :, piece] = rounded[rows:]
-        seen = rounded.astype(jnp.float32)
-        stats[0:1, piece] = jnp.max(seen, axis=0, keepdims=True)
-        stats[1:2, piece] = -jnp.min(seen, axis=0, keepdims=True)
+        part = dot_nn(lhs[:, piece], head[piece])
+        if s:
+            part = acc[...] + part
+        if s < slabs - 1:
+            acc[...] = part
+        for d in range(s * slab // block, (s + 1) * slab // block):
+            for i in range(2):
+                sent_feats[i, d // n_group, d % n_group] = lhs[
+                    i * rows : (i + 1) * rows, d * block : (d + 1) * block
+                ].T
+    rounded = part.astype(jnp.bfloat16)
+    proj[0] = rounded[:rows]
+    proj[1] = rounded[rows:]
+    seen = rounded.astype(jnp.float32)
+    stats[0:1] = jnp.max(seen, axis=0, keepdims=True)
+    stats[1:2] = -jnp.min(seen, axis=0, keepdims=True)
     pl.semaphore_wait(barrier, len(peers))
 
     for k in range(1, n_dp):
@@ -564,12 +575,6 @@
             arrived(landed, r_dp.at[i, source])
         return source
 
-    def turn(i):
-        for d in range(n_dp * n_group):
-            sent_feats[i, d // n_group, d % n_group] = lhs[
-                i * rows : (i + 1) * rows, d * block : (d + 1) * block
-            ].T
-
     def send_feats(i, which):
         for m, target in enumerate(others):
             if m in which:
@@ -583,7 +588,6 @@
     for k in range(1, n_dp):
         send(ids_own, ids_in.at[k], s_ids.at[k], r_ids.at[k], (dp_at(k), me_g))
 
-    turn(1)
     bounds = stats[...]
     for k in range(1, n_dp):
         arrived(stats_dp.at[k], r_stat_d.at[k])
@@ -593,7 +597,6 @@
         send(stats_mid, stats_group.at[k], s_stat_g.at[k], r_stat_g.at[k], (me_d, group_at(k)))
     send_feats(1, range(chips))
     relay(0, 1)
-    lower(0)
     for k in range(1, n_group):
         arrived(stats_group.at[k], r_stat_g.at[k])
         bounds = jnp.maximum(bounds, stats_group[k])
@@ -618,8 +621,8 @@
             arrived(landed, r_batch.at[i, source])
             send(landed, landed, s_batch.at[i, chips + m], r_batch.at[i, source], (me_d, partner))
 
+    over(1, z, batch.at[1, me_g])
     send_feats(1, range(chips, n_group))
-    turn(0)
     stay = [
         pltpu.make_async_copy(
             sent_feats.at[i, :, me_g], turned.at[i, :, :, own_rows(me_g)], l_own.at[i]
@@ -649,15 +652,15 @@
         score = dot_nt(block_emb, query) / scaling_divisor
         hard_exp[source] = jnp.where(named(ids_own[...], source), jnp.exp(score), 0.0)
 
-    hard_scores(across)
     if line > 2:
         relay(0, 2)
+    lower(0)
     along(1, z, batch.at[1, me_g], True, True)
+    hard_scores(across)
     hand_over(0)
     send_feats(0, range(chips))
     for s in range(3, line):
         relay(0, s)
-    over(1, z, batch.at[1, me_g])
     hand_over(1)
 
     for source in [partner] + relayed:
@@ -675,7 +678,6 @@
     for k in range(1, line):
         hard_scores(plane(k) * inner + y)
     relay(1, 1)
-    lower(1)
     for k in range(1, line):
         hard_scores(gathered(0, k))
 
@@ -706,6 +708,9 @@
     send_feats(0, range(chips, n_group))
     if line > 2:
         relay(1, 2)
+    lower(1)
+    for s in range(3, line):
+        relay(1, s)
 
     for source in [partner] + relayed:
         arrived(batch.at[1, source], r_batch.at[1, source])
@@ -728,8 +733,6 @@
         return dot_nn(chosen, hard)
 
     grad += hard_back(across)
-    for s in range(3, line):
-        relay(1, s)
     for m, source in enumerate(beside):
         landed = dy.at[1, own_rows(source)]
         arrived(landed, r_dyq.at[source])
@@ -769,42 +772,49 @@
             arrived(dy.at[0, own_rows(source), columns(c)], r_dyp.at[c, source])
         part = dot_nn(seen_rows(0), dy[0, :, columns(c)]).reshape(n_dp, block, wide)
         total[c] = part + (total[c] if c < early else from_query(c))
-        for at in range(line):
-            pair_out[c, at] = total[c, at * inner + 1 - y].astype(jnp.bfloat16)
-        send(pair_out.at[c], pair_in.at[c], s_p.at[c], r_p.at[c], (across, me_g))
+        for j in [*range(1, line), 0]:
+            pair_out[c, j] = total[c, z_at(j) * inner + 1 - y].astype(jnp.bfloat16)
+            send(pair_out.at[c, j], pair_in.at[c, j], s_p.at[c, j], r_p.at[c, j], (across, me_g))
 
     def second(c):
-        arrived(pair_in.at[c], r_p.at[c])
-        summed = lambda at: total[c, at * inner + y] + pair_in[c, at].astype(jnp.float32)
-        for j in range(1, line):
-            line_out[c, j] = summed(z_at(j)).astype(jnp.bfloat16)
-            send(
-                line_out.at[c, j], line_in.at[c, j], s_l.at[c, j], r_l.at[c, j],
-                (z_at(j) * inner + y, me_g),
-            )
-        kept[c] = summed(z)
+        for j in [*range(1, line), 0]:
+            arrived(pair_in.at[c, j], r_p.at[c, j])
+            value = total[c, z_at(j) * inner + y] + pair_in[c, j].astype(jnp.float32)
+            if j:
+                line_out[c, j] = value.astype(jnp.bfloat16)
+                send(
+                    line_out.at[c, j], line_in.at[c, j], s_l.at[c, j], r_l.at[c, j],
+                    (z_at(j) * inner + y, me_g),
+                )
+            else:
+                kept[c] = value
+
+    def leave(c):
+        return pltpu.make_async_copy(kept.at[c], out.at[:, columns(c)], l_out.at[c])
 
     def third(c):
         value = kept[c]
         for j in range(1, line):
             arrived(line_in.at[c, j], r_l.at[c, j])
             value += line_in[c, j].astype(jnp.float32)
-        out[:, columns(c)] = value
+        kept[c] = value
+        leave(c).start()
 
     lag = 3
     for source in others:
         arrived(turned.at[0, :, :, own_rows(source)], r_feat.at[0, source])
     pass_on(0)
-    for c in range(chunks):
+    for c in range(chunks + lag + 2):
         if c + 1 < chunks:
             pass_on(c + 1)
-        first(c)
-        if c >= lag:
+        if c < chunks:
+            first(c)
+        if 0 <= c - lag < chunks:
             second(c - lag)
-    for c in range(max(0, chunks - lag), chunks):
-        second(c)
+        if 0 <= c - lag - 2 < chunks:
+            third(c - lag - 2)
     for c in range(chunks):
-        third(c)
+        leave(c).wait()
     for condition, copy in unsent:
         if condition is None:
             copy.wait_send()
@@ -817,7 +827,7 @@
     emb = head.shape[1]
     line, chips = n_dp // 2, n_group // 2
     chunks = emb // 128
-    slabs = max(1, emb // 256)
+    slabs = max(1, width // max(512, block))
     wide = emb // chunks
     bf16 = lambda *shape: pltpu.VMEM(shape, jnp.bfloat16)
     f32 = lambda *shape: pltpu.VMEM(shape, jnp.float32)
@@ -832,9 +842,9 @@
             jax.ShapeDtypeStruct((1, rows), jnp.float32),
         ),
         in_specs=[anywhere, anywhere, anywhere, VMEM],
-        out_specs=(VMEM, VMEM),
+        out_specs=(anywhere, VMEM),
         scratch_shapes=[
-            bf16(2 * rows, width), bf16(width, emb), bf16(2, rows, emb),
+            bf16(2 * rows, width), bf16(width, emb), f32(2 * rows, emb), bf16(2, rows, emb),
             f32(2, emb), f32(n_dp, 2, emb), f32(2, emb), f32(n_group, 2, emb),
             i32(8, rows), i32(n_dp, 8, rows),
             f32(2, rows, emb), f32(2, rows, 1), bf16(2, n_group, rows, emb),
@@ -849,14 +859,14 @@
             bf16(chunks, line, block, wide), bf16(chunks, line, block, wide),
             f32(chunks, block, wide),
         ]
-        + sems(2) + sems(slabs) + sems(2) + pairs(n_dp) + pairs(n_group) + pairs(n_dp)
+        + sems(2, slabs) + sems(slabs) + sems(2) + sems(chunks) + pairs(n_dp) + pairs(n_group) + pairs(n_dp)
         + sems(2, 2, line) + sems(2, line) + sems(2, n_dp) + pairs(2)
         + sems(2, 2 * chips) + sems(2, n_group)
         + sems(2, n_group) + sems(2, n_group)
         + pairs(n_group) + pairs(n_dp)
         + sems(2 * chips) + sems(n_group)
         + sems(chunks, 2 * chips) + sems(chunks, n_group)
-        + pairs(chunks) + pairs(chunks, line),
+        + pairs(chunks, line) + pairs(chunks, line),
         compiler_params=pltpu.CompilerParams(
             has_side_effects=True, collective_id=0, vmem_limit_bytes=60 * 2**20
         ),

time: 107 us -> 96.9 us (0.906)
  Pallas kernels: 103 us -> 93.1 us
    pallas_call x1, Pallas kernels: 103 us -> 93.1 us  [chip_step(): pl.pallas_call(functools.partial(chip_kernel, n_dp, n_group, chunks, slab...]
where the time goes in v3:
time: 96.9 us; the launch traced here: 96.7 us
  Pallas kernels  93.1 us (96%)
  local copies, waits for them, and re-layouts  2.99 us (3%)
    pallas_call x1, Pallas kernels, chip_step(): pl.pallas_call(functools.partial(chip_kernel, n_dp, n_group, chunks, slab...  93.1 us
    unnamed x2, local copies, waits for them, and re-layouts  2.99 us

profile of v3, /device:TPU:0, one launch (start us, length us, event | category | flops | bytes accessed | tf_op | source)
XLA Modules:
  0.0 96.7 jit_solution(1561644872561358814)
XLA Ops:
  0.6 93.1 %chip_step.1 = (f32[128,1024]{1,0:T(8,128)}, f32[1,128]{1,0:T(1,128)}) custom-call(bf16[128,4096]{1,0:T(8,128)(2,1)} %pass_hbm.1, bf16[128,4096]{1,0:T(8,128)(2,1)} %query_hbm.1, bf16[4096,1024]{1,0:T(8,128)(2,1)} %head_hbm.1, s32[7,128]{1,0:T(8,128)} %bitcast.2), custom_call_target="tpu_custom_call" | custom-call | tf_op jit(solution)/shard_map/chip_step/pallas_call | solution.py:838
  93.7 1.9 %copy.8 = f32[128,1024]{1,0:T(8,128)} copy(f32[128,1024]{1,0:T(8,128)} %get-tuple-element.8) | data formatting | bytes 1048576
  95.6 1.1 %copy.9 = f32[128]{0:T(128)} copy(f32[128]{0:T(128)} %bitcast.3) | data formatting | bytes 1024
